TPU v7x, 256 devices: a whole 4x4x8 slice. The times are simulated.
256 devices in a mesh: tok: 32 (over z, y_hi, core), row: 2 (over y_lo), col: 4 (over x).
Axes of the slice: x: 4, y: 4 (y_hi: 2, y_lo: 2; y = y_hi * 2 + y_lo), z: 8, core: 2. Of those that a mesh axis runs over, the one named last changes fastest.
Arguments:
- activations: bfloat16 [11264, 4096], P(('tok', 'row'), 'col'), may hold values from -512 to 512
- norm_gain: bfloat16 [4096], P('col'), may hold values from 1.5 to 10
- qkv_weight: bfloat16 [4096, 16, 384], P('row', 'col'), may hold values from -0.09375 to 0.09375
- doc_ids: int32 [11264], P(('tok', 'row')), may hold values from 0 to 3, never falling along the last dimension, each value on 1 to 8448 neighbouring positions
Outputs:
- attended: bfloat16 [11264, 2048], P(('tok', 'row'), 'col')
Inputs may be any that keep to these rules, and one draw needn't show every extreme that they name: `doc_ids`: never falls along the sequence; each of the 4 documents holds 1 to 8448 tokens and one holds exactly 8448.
All inputs are finite; a program needn't handle non-finite values.
Results may differ from a plain program's by a relative error of at most 0.007.
The roundings to bfloat16 on the way count: a program that leaves them out, or rounds other values in their place, can miss the bound.
Values may be sent and summed in bfloat16 or wider, within the bound.
A program may use at most 128 MiB of HBM per device.

v0:
```python
import math
import jax
import jax.numpy as jnp
from jax import lax
from jax.sharding import PartitionSpec as P


def rotate(vectors, places):
    half = vectors.shape[-1] // 2
    spacing = jnp.arange(half).astype(jnp.float32) * (2.0 / vectors.shape[-1])
    inverse = jnp.power(10000.0, -spacing)
    angles = places.astype(jnp.float32)[:, None] * inverse[None, :]
    cosine = jnp.cos(angles)[:, None, :]
    sine = jnp.sin(angles)[:, None, :]
    first_half = vectors[..., :half]
    second_half = vectors[..., half:]
    return jnp.concatenate(
        [first_half * cosine - second_half * sine, first_half * sine + second_half * cosine],
        axis=-1,
    )


def per_device(activations, norm_gain, qkv_weight, doc_ids):
    row_count = activations.shape[0]
    whole, gain_whole = (
        lax.all_gather(activations, "col", axis=1, tiled=True),
        lax.all_gather(norm_gain, "col", axis=0, tiled=True),
    )
    widened = whole.astype(jnp.float32)
    mean_square = jnp.mean(widened * widened, axis=1, keepdims=True)
    normed = (widened * lax.rsqrt(mean_square + 1e-05) * gain_whole.astype(jnp.float32)).astype(
        jnp.bfloat16
    )
    span, local_heads, width = qkv_weight.shape
    head_size = width // 3
    flat_weight = qkv_weight.reshape(span, local_heads * width)
    projected = jnp.dot(
        normed,
        lax.all_gather(flat_weight, "row", axis=0, tiled=True),
        preferred_element_type=jnp.float32,
    )
    projected = projected.reshape(row_count, local_heads, width)
    first = (lax.axis_index("tok") * lax.axis_size("row") + lax.axis_index("row")) * row_count
    places = first + jnp.arange(row_count, dtype=jnp.int32)
    query = rotate(projected[..., :head_size], places).astype(jnp.bfloat16)
    keys = rotate(projected[..., head_size : 2 * head_size], places).astype(jnp.bfloat16)
    values = projected[..., 2 * head_size :].astype(jnp.bfloat16)
    scale = 1.0 / math.sqrt(head_size)

    def update(state, block_keys, block_values, block_docs, key_places):
        running, totals, summed = state
        scores = (
            jnp.einsum("qhd,khd->hqk", query, block_keys, preferred_element_type=jnp.float32)
            * scale
        )
        visible = (key_places[None, None, :] <= places[None, :, None]) & (
            block_docs[None, None, :] == doc_ids[None, :, None]
        )
        masked = jnp.where(visible, scores, -jnp.inf)
        newest = jnp.maximum(running, jnp.max(masked, axis=2))
        factor = jnp.exp(running - newest)
        exponentials = jnp.where(visible, jnp.exp(masked - newest[:, :, None]), 0.0)
        weights = exponentials.astype(jnp.bfloat16)
        totals = totals * factor + jnp.sum(exponentials, axis=2)
        summed = summed * factor.T[:, :, None] + jnp.einsum(
            "hqk,khd->qhd", weights, block_values, preferred_element_type=jnp.float32
        )
        return (newest, totals, summed)

    initial = (
        jnp.full((local_heads, row_count), -1e30, jnp.float32),
        jnp.zeros((local_heads, row_count), jnp.float32),
        jnp.zeros((row_count, local_heads, head_size), jnp.float32),
    )
    pair_keys, pair_values, pair_docs = (
        lax.all_gather(keys, "row", axis=0, tiled=True),
        lax.all_gather(values, "row", axis=0, tiled=True),
        lax.all_gather(doc_ids, "row", axis=0, tiled=True),
    )
    state = initial
    block_keys = lax.all_gather(pair_keys, "tok", axis=0, tiled=True)
    block_values = lax.all_gather(pair_values, "tok", axis=0, tiled=True)
    block_docs = lax.all_gather(pair_docs, "tok", axis=0, tiled=True)
    count = block_keys.shape[0]
    key_places = jnp.arange(count, dtype=jnp.int32)
    rounds = count // 1024
    stacked = (
        block_keys.reshape(rounds, 1024, local_heads, head_size),
        block_values.reshape(rounds, 1024, local_heads, head_size),
        block_docs.reshape(rounds, 1024),
        key_places.reshape(rounds, 1024),
    )

    def advance(carried, blocks):
        return (update(carried, blocks[0], blocks[1], blocks[2], blocks[3]), None)

    state, unused = lax.scan(advance, state, stacked)
    running, totals, summed = state
    attended = summed / totals.T[:, :, None]
    return attended.reshape(row_count, local_heads * head_size).astype(jnp.bfloat16)


def solution(mesh):
    placed = (P(("tok", "row"), "col"), P("col"), P("row", "col", None), P(("tok", "row")))
    return jax.shard_map(
        per_device, mesh=mesh, in_specs=placed, out_specs=P(("tok", "row"), "col"), check_vma=False
    )
```

profile of v0, /device:TPU:1, one launch (start us, length us, event | category | flops | bytes accessed | tf_op | source)
XLA Modules:
  0.0 528.5 jit_solution(10905290454342149251)
XLA Ops:
  6.5 0.7 all-gather.5.cloned.1.call-update
  7.3 6.6 %copy.35 = bf16[256,8,4,384]{3,1,2,0:T(8,128)(2,1)} copy(bf16[256,8,4,384]{3,2,1,0:T(4,128)(2,1)} %bitcast.72) | data formatting | bytes 12582912
  13.9 0.6 copy-done.1
  14.5 9.3 %all_gather.30 = bf16[4096]{0:T(1024)(128)(2,1)S(1)} all-gather(bf16[1024]{0:T(1024)(128)(2,1)S(1)} %copy-done.1), channel_id=1, replica_groups=mesh['tok'=32,'row'=2,'col'=4] {'col'}, dimensions={0}, use_global_device_ids=true | all-gather | bytes 10240 | tf_op jit(solution)/shard_map/all_gather | solution.py:27
  23.9 0.4 multiply_cosine_fusion
  24.3 16.4 %all-gather.5.cloned.1.call-done = bf16[176,4096]{1,0:T(8,128)(2,1)} async-done(((bf16[176,1024]{1,0:T(8,128)(2,1)}), bf16[176,4096]{1,0:T(8,128)(2,1)}) %all-gather.5.cloned.1.call-update) | async-done | bytes 1441808 | tf_op jit(solution)/shard_map/all_gather | solution.py:26
  40.7 1.7 fusion.26
  42.4 158.1 %all-gather.7.cloned.1.call-done = bf16[4096,1536]{1,0:T(8,128)(2,1)} async-done(((bf16[2048,1536]{1,0:T(8,128)(2,1)}), bf16[4096,1536]{1,0:T(8,128)(2,1)}) %all-gather.7.cloned.1.call-update) | async-done | bytes 12582928 | tf_op jit(solution)/shard_map/all_gather | solution.py:39
  200.5 7.5 %fusion.29 = f32[176,1536]{1,0:T(8,128)S(1)} fusion(bf16[4096,1536]{1,0:T(8,128)(2,1)} %all-gather.7.cloned.1.call-done, bf16[176,4096]{1,0:T(8,128)(2,1)} %all-gather.5.cloned.1.call-done, f32[4096]{0:T(1024)S(1)} %convert_element_type.38, f32[176]{0:T(256)S(1)} %add_rsqrt_fusion), kind=kOutput, calls=%fused_computation.35 | convolution fusion | flops 2217476096 | bytes 15123136 | tf_op jit(solution)/shard_map/dot_general | solution.py:37
  208.4 0.5 fusion.34
  209.3 6.0 %all_gather.32 = bf16[352,4,128]{2,0,1:T(8,128)(2,1)} all-gather(bf16[176,4,128]{2,0,1:T(8,128)(2,1)S(1)} %pad_maximum_fusion), channel_id=1, replica_groups=mesh['tok'=32,'row'=2,'col'=4] {'row'}, dimensions={0}, use_global_device_ids=true | all-gather | bytes 540672 | tf_op jit(solution)/shard_map/all_gather | solution.py:76
  215.5 5.1 all_gather.34
  220.7 0.6 dynamic-slice
  221.3 0.6 dynamic-slice.1
  223.3 3.1 all-reduce
  226.7 129.4 %all-reduce.1 = s32[11264]{0:T(1024)S(1)} all-reduce(s32[11264]{0:T(1024)S(1)} %dynamic-update-slice.1), channel_id=1, replica_groups=mesh['tok'=32,'row'=2,'col'=4] {'tok'}, use_global_device_ids=true, to_apply=%add.1 | all-reduce | flops 11264 | bytes 90112
  356.1 0.6 multiply_add_fusion
  356.9 86.2 %all-gather.11.cloned.1.call-done = bf16[11264,4,128]{2,0,1:T(8,128)(2,1)} async-done(((bf16[352,4,128]{2,0,1:T(8,128)(2,1)}), bf16[11264,4,128]{2,0,1:T(8,128)(2,1)}) %all-gather.11.cloned.1.call-update) | async-done | bytes 11534352 | tf_op jit(solution)/shard_map/all_gather | solution.py:82
  443.1 77.1 %while.15 = (s32[]{:T(128)}, f32[4,176]{1,0:T(4,128)S(1)}, f32[4,176]{1,0:T(4,128)S(1)}, f32[176,4,128]{2,0,1:T(8,128)}, s32[11,1024]{1,0:T(8,128)}, /*index=5*/...) while((s32[]{:T(128)}, f32[4,176]{1,0:T(4,128)S(1)}, ...), condition=%wide.region_4.5_spmd.clone, body=%wide.region_1.4_spmd.clone.sunk | while | flops 379285824 | bytes 12442833 | solution.py:97
  443.1 0.8 constant_dynamic-slice_fusion.3
  444.1 2.0 fusion.49
  446.1 2.9 fusion.53
  449.0 1.0 fusion.51
  450.0 0.8 constant_dynamic-slice_fusion.3
  451.0 2.0 fusion.49
  453.0 3.0 fusion.53
  456.0 1.0 fusion.51
  457.0 0.8 constant_dynamic-slice_fusion.3
  458.0 2.0 fusion.49
  460.0 3.0 fusion.53
  463.0 1.0 fusion.51
  464.1 0.8 constant_dynamic-slice_fusion.3
  465.1 2.0 fusion.49
  467.0 3.0 fusion.53
  470.1 1.0 fusion.51
  471.1 0.8 constant_dynamic-slice_fusion.3
  472.1 2.0 fusion.49
  474.1 3.0 fusion.53
  477.1 1.0 fusion.51
  478.1 0.8 constant_dynamic-slice_fusion.3
  479.1 2.0 fusion.49
  481.1 3.0 fusion.53
  484.1 1.0 fusion.51
  485.1 0.8 constant_dynamic-slice_fusion.3
  486.1 2.0 fusion.49
  488.1 3.0 fusion.53
  491.1 1.0 fusion.51
  492.1 0.8 constant_dynamic-slice_fusion.3
  493.1 2.0 fusion.49
  495.1 3.0 fusion.53
  498.1 1.0 fusion.51
  499.1 0.8 constant_dynamic-slice_fusion.3
  500.1 2.0 fusion.49
  502.1 3.0 fusion.53
  505.1 1.0 fusion.51
  506.1 0.8 constant_dynamic-slice_fusion.3
  507.1 2.0 fusion.49
  509.1 3.0 fusion.53
  512.1 1.0 fusion.51
  513.2 0.8 constant_dynamic-slice_fusion.3
  514.2 2.0 fusion.49
  516.1 3.0 fusion.53
  519.2 1.0 fusion.51
  520.2 1.8 copy_bitcast_fusion
  (88 shorter events, 4.4 us)
Async XLA Ops:
  6.5 34.2 %all-gather.5.cloned.1.call-start = ((), (), s32[]{:S(2)}) async-start(), calls=%async_computation | async-start | bytes 1802240 | tf_op jit(solution)/shard_map/all_gather | solution.py:26
  7.3 193.3 %all-gather.7.cloned.1.call-start = ((), (), s32[]{:S(2)}) async-start(), calls=%async_computation.1 | async-start | bytes 18874368 | tf_op jit(solution)/shard_map/all_gather | solution.py:39
  13.9 0.7 copy-start.1
  13.9 343.0 %all-gather.9.cloned.1.call-start = ((), (), s32[]{:S(2)}) async-start(), calls=%async_computation.2 | async-start | bytes 11894784 | tf_op jit(solution)/shard_map/all_gather | solution.py:81
  208.9 11.8 %copy-start.3 = (u32[256]{0:T(256)S(1)}, u32[256]{0:T(256)}, u32[]{:S(2)}) copy-start(u32[256]{0:T(256)} %constant.56) | copy-start | bytes 3076
  208.9 12.4 %copy-start.2 = (u32[256]{0:T(256)S(1)}, u32[256]{0:T(256)}, u32[]{:S(2)}) copy-start(u32[256]{0:T(256)} %constant.61) | copy-start | bytes 3076
  208.9 14.1 %copy-start = (s32[176]{0:T(256)S(1)}, s32[176]{0:T(256)}, u32[]{:S(2)}) copy-start(s32[176]{0:T(256)} %param.9) | copy-start | bytes 2116
  215.3 227.8 %all-gather.11.cloned.1.call-start = ((), (), s32[]{:S(2)}) async-start(), calls=%async_computation.3 | async-start | bytes 11894784 | tf_op jit(solution)/shard_map/all_gather | solution.py:82
Sparse Core Ops, SparseCore 0:
  9.1 31.5 all-gather.4
  42.5 157.9 all-gather.6
  215.4 115.8 all-gather.8
  334.0 109.0 all-gather.10
where the time goes:
time: 530 us; the launch traced here: 529 us
  waiting for transfers between devices  262 us (49%)
  blocking collectives  153 us (29%)
  matrix products  62.1 us (12%)
  other arithmetic  18.5 us (3%)
  local copies, waits for them, and re-layouts  18.3 us (3%)
  between operations  14.5 us (3%)
    all_gather x1, waiting for transfers between devices, per_device(): lax.all_gather(flat_weight, 'row', axis=0, tiled=True)  158 us
    unnamed x2, blocking collectives  132 us
    all_gather x1, waiting for transfers between devices, per_device(): block_values = lax.all_gather(pair_values, 'tok', axis=0, tiled=True)  86.2 us
    dot_general x11, matrix products, update(): jnp.einsum('hqk,khd->qhd', weights, block_values, preferred_element_type=...  33 us
    dot_general x11, matrix products, update(): jnp.einsum('qhd,khd->hqk', query, block_keys, preferred_element_type=jnp....  21.6 us
    all_gather x1, waiting for transfers between devices, per_device(): lax.all_gather(activations, 'col', axis=1, tiled=True)  16.4 us
    reduce_sum x11, other arithmetic, update(): totals = totals * factor + jnp.sum(exponentials, axis=2)  10.7 us
  transfers between devices with their start and end apart: 4, of which 3 were waited for; matrix products, arithmetic and copies ran while one was open for 2% of the time, Pallas kernels for 0%

commit v1 on v0

--- a/solution.py
+++ b/solution.py
@@ -3,6 +3,7 @@
 import jax.numpy as jnp
 from jax import lax
 from jax.sharding import PartitionSpec as P
+from jax.lax import all_to_all, axis_size
 
 
 def rotate(vectors, places):
@@ -23,7 +24,15 @@
 def per_device(activations, norm_gain, qkv_weight, doc_ids):
     row_count = activations.shape[0]
     whole, gain_whole = (
-        lax.all_gather(activations, "col", axis=1, tiled=True),
+        jnp.concatenate(
+            all_to_all(
+                jnp.stack([activations for _ in range(axis_size("col"))], 0),
+                split_axis=0,
+                axis_name="col",
+                concat_axis=0,
+            ),
+            1,
+        ),
         lax.all_gather(norm_gain, "col", axis=0, tiled=True),
     )
     widened = whole.astype(jnp.float32)

time: 530 us -> 508 us (0.958)
  waiting for transfers between devices: 262 us -> 217 us
  blocking collectives: 153 us -> 164 us
  local copies, waits for them, and re-layouts: 18.3 us -> 25.4 us
    all_gather x1, waiting for transfers between devices: 158 us -> 131 us  [per_device(): lax.all_gather(flat_weight, 'row', axis=0, tiled=True)]
    all_gather x1 -> x0, waiting for transfers between devices: 16.4 us -> none  [per_device(): lax.all_gather(activations, 'col', axis=1, tiled=True)]
    all_gather x1, blocking collectives: 9.3 us -> 20.1 us  [per_device(): lax.all_gather(norm_gain, 'col', axis=0, tiled=True)]
    reshape x1, local copies, waits for them, and re-layouts: 0.37 us -> 10.6 us  [per_device(): flat_weight = qkv_weight.reshape(span, local_heads * width)]
    unnamed x16, local copies, waits for them, and re-layouts: 8.87 us -> 2.76 us
  transfers between devices with their start and end apart: 4 -> 4, of which waited for: 3 -> 2; matrix products, arithmetic and copies ran while one was open for 2% -> 1% of each run, Pallas kernels for 0% -> 0%
where the time goes in v1:
time: 508 us; the launch traced here: 506 us
  waiting for transfers between devices  217 us (43%)
  blocking collectives  164 us (32%)
  matrix products  61.8 us (12%)
  local copies, waits for them, and re-layouts  25.4 us (5%)
  other arithmetic  17.8 us (4%)
  between operations  14.6 us (3%)
    unnamed x2, blocking collectives  133 us
    all_gather x1, waiting for transfers between devices, per_device(): lax.all_gather(flat_weight, 'row', axis=0, tiled=True)  131 us
    all_gather x1, waiting for transfers between devices, per_device(): block_values = lax.all_gather(pair_values, 'tok', axis=0, tiled=True)  86.2 us
    dot_general x11, matrix products, update(): jnp.einsum('hqk,khd->qhd', weights, block_values, preferred_element_type=...  32.9 us
    dot_general x11, matrix products, update(): jnp.einsum('qhd,khd->hqk', query, block_keys, preferred_element_type=jnp....  21.6 us
    all_gather x1, blocking collectives, per_device(): lax.all_gather(norm_gain, 'col', axis=0, tiled=True)  20.1 us
    reduce_sum x11, other arithmetic, update(): totals = totals * factor + jnp.sum(exponentials, axis=2)  10.7 us
    reshape x1, local copies, waits for them, and re-layouts, per_device(): flat_weight = qkv_weight.reshape(span, local_heads * width)  10.6 us
  transfers between devices with their start and end apart: 4, of which 2 were waited for; matrix products, arithmetic and copies ran while one was open for 1% of the time, Pallas kernels for 0%

profile of v1, /device:TPU:1, one launch (start us, length us, event | category | flops | bytes accessed | tf_op | source)
XLA Modules:
  0.0 505.6 jit_solution(15897941157685381817)
XLA Ops:
  6.5 10.6 %copy.18 = bf16[2048,4,384]{0,2,1:T(8,128)(2,1)} copy(bf16[2048,4,384]{2,1,0:T(4,128)(2,1)} %param.8) | data formatting | bytes 12582912 | tf_op jit(solution)/shard_map/reshape | solution.py:45
  17.2 1.0 copy-done
  18.2 1.3 stack.2
  19.5 4.8 all-to-all-start
  24.3 20.1 %all_gather.26 = bf16[4096]{0:T(1024)(128)(2,1)S(1)} all-gather(bf16[1024]{0:T(1024)(128)(2,1)S(1)} %copy-done.2), channel_id=1, replica_groups=mesh['tok'=32,'row'=2,'col'=4] {'col'}, dimensions={0}, use_global_device_ids=true | all-gather | bytes 10240 | tf_op jit(solution)/shard_map/all_gather | solution.py:36
  45.2 0.5 fusion.29
  45.8 1.1 copy.13
  46.9 1.1 reshape.200
  48.0 130.6 %all-gather.4.cloned.1.call-done = bf16[4096,1536]{0,1:T(8,128)(2,1)} async-done(((bf16[2048,1536]{0,1:T(8,128)(2,1)}), bf16[4096,1536]{0,1:T(8,128)(2,1)}) %all-gather.4.cloned.1.call-update) | async-done | bytes 12582928 | tf_op jit(solution)/shard_map/all_gather | solution.py:48
  178.6 7.3 %fusion.31 = f32[176,4,384]{2,0,1:T(8,128)S(1)} fusion(bf16[176,4096,1]{1,0,2:T(8,128)(2,1)S(1)} %reshape.200, bf16[4,384,4096]{2,1,0:T(8,128)(2,1)} %bitcast.79), kind=kOutput, calls=%fused_computation.52 | convolution fusion | flops 2214592512 | bytes 15106048 | tf_op jit(solution)/shard_map/dot_general | solution.py:46
  186.4 6.0 %all_gather.28 = bf16[352,4,128]{2,0,1:T(8,128)(2,1)} all-gather(bf16[176,4,128]{2,0,1:T(8,128)(2,1)S(1)} %pad_maximum_fusion), channel_id=1, replica_groups=mesh['tok'=32,'row'=2,'col'=4] {'row'}, dimensions={0}, use_global_device_ids=true | all-gather | bytes 540672 | tf_op jit(solution)/shard_map/all_gather | solution.py:85
  192.5 5.1 %all_gather.30 = bf16[352,4,128]{2,0,1:T(8,128)(2,1)} all-gather(bf16[176,4,128]{2,0,1:T(8,128)(2,1)S(1)} %slice.41), channel_id=1, replica_groups=mesh['tok'=32,'row'=2,'col'=4] {'row'}, dimensions={0}, use_global_device_ids=true | all-gather | bytes 540672 | tf_op jit(solution)/shard_map/all_gather | solution.py:86
  197.7 0.6 dynamic-slice
  198.3 0.7 dynamic-slice.1
  200.6 3.1 all-reduce
  204.0 129.4 %all-reduce.1 = s32[11264]{0:T(1024)S(1)} all-reduce(s32[11264]{0:T(1024)S(1)} %dynamic-update-slice.1), channel_id=1, replica_groups=mesh['tok'=32,'row'=2,'col'=4] {'tok'}, use_global_device_ids=true, to_apply=%add.1 | all-reduce | flops 11264 | bytes 90112
  333.4 0.6 multiply_add_fusion
  334.2 86.2 %all-gather.8.cloned.1.call-done = bf16[11264,4,128]{2,0,1:T(8,128)(2,1)} async-done(((bf16[352,4,128]{2,0,1:T(8,128)(2,1)}), bf16[11264,4,128]{2,0,1:T(8,128)(2,1)}) %all-gather.8.cloned.1.call-update) | async-done | bytes 11534352 | tf_op jit(solution)/shard_map/all_gather | solution.py:91
  420.3 76.9 %while.15 = (s32[]{:T(128)}, f32[4,176]{1,0:T(4,128)S(1)}, f32[4,176]{1,0:T(4,128)S(1)}, f32[176,4,128]{2,0,1:T(8,128)}, s32[11,1024]{1,0:T(8,128)}, /*index=5*/...) while((s32[]{:T(128)}, f32[4,176]{1,0:T(4,128)S(1)}, ...), condition=%wide.region_4.5_spmd.clone, body=%wide.region_1.4_spmd.clone.sunk | while | flops 379285824 | bytes 12442833 | solution.py:106
  420.3 0.8 constant_dynamic-slice_fusion.3
  421.3 2.0 fusion.47
  423.3 2.9 fusion.51
  426.2 1.0 fusion.49
  427.3 0.8 constant_dynamic-slice_fusion.3
  428.3 2.0 fusion.47
  430.2 3.0 fusion.51
  433.2 1.0 fusion.49
  434.3 0.8 constant_dynamic-slice_fusion.3
  435.3 2.0 fusion.47
  437.2 3.0 fusion.51
  440.2 1.0 fusion.49
  441.3 0.8 constant_dynamic-slice_fusion.3
  442.3 2.0 fusion.47
  444.2 3.0 fusion.51
  447.2 1.0 fusion.49
  448.3 0.8 constant_dynamic-slice_fusion.3
  449.3 2.0 fusion.47
  451.2 3.0 fusion.51
  454.2 1.0 fusion.49
  455.3 0.8 constant_dynamic-slice_fusion.3
  456.3 2.0 fusion.47
  458.2 3.0 fusion.51
  461.2 1.0 fusion.49
  462.3 0.8 constant_dynamic-slice_fusion.3
  463.2 2.0 fusion.47
  465.2 3.0 fusion.51
  468.2 1.0 fusion.49
  469.2 0.8 constant_dynamic-slice_fusion.3
  470.2 2.0 fusion.47
  472.2 3.0 fusion.51
  475.2 1.0 fusion.49
  476.2 0.8 constant_dynamic-slice_fusion.3
  477.2 2.0 fusion.47
  479.2 3.0 fusion.51
  482.2 1.0 fusion.49
  483.2 0.8 constant_dynamic-slice_fusion.3
  484.2 2.0 fusion.47
  486.2 3.0 fusion.51
  489.2 1.0 fusion.49
  490.2 0.8 constant_dynamic-slice_fusion.3
  491.2 2.0 fusion.47
  493.2 3.0 fusion.51
  496.2 1.0 fusion.49
  497.2 1.8 copy_bitcast_fusion
  (90 shorter events, 4.8 us)
Async XLA Ops:
  6.5 172.0 %all-gather.4.cloned.1.call-start = ((), (), s32[]{:S(2)}) async-start(), calls=%async_computation.1 | async-start | bytes 18874368 | tf_op jit(solution)/shard_map/all_gather | solution.py:48
  17.2 1.0 copy-start
  18.2 6.1 %copy-start.2 = (bf16[1024]{0:T(1024)(128)(2,1)S(1)}, bf16[1024]{0:T(1024)(128)(2,1)}, u32[]{:S(2)}) copy-start(bf16[1024]{0:T(1024)(128)(2,1)} %param.7) | copy-start | bytes 6148
  19.5 25.4 %all-to-all-start = ((bf16[4,176,1024]{2,1,0:T(8,128)(2,1)}), bf16[4,176,1024]{2,1,0:T(8,128)(2,1)S(1)}, u32[]{:S(2)}, u32[]{:S(2)}) async-start(bf16[4,176,1024]{2,1,0:T(8,128)(2,1)} %stack.2), calls=%async_computation | async-start | bytes 2883584 | tf_op jit(solution)/shard_map/all_to_all | solution.py:28
  24.3 309.9 %all-gather.6.cloned.1.call-start = ((), (), s32[]{:S(2)}) async-start(), calls=%async_computation.2 | async-start | bytes 11894784 | tf_op jit(solution)/shard_map/all_gather | solution.py:90
  185.9 11.8 %copy-start.4 = (u32[256]{0:T(256)S(1)}, u32[256]{0:T(256)}, u32[]{:S(2)}) copy-start(u32[256]{0:T(256)} %constant.56) | copy-start | bytes 3076
  185.9 12.4 %copy-start.3 = (u32[256]{0:T(256)S(1)}, u32[256]{0:T(256)}, u32[]{:S(2)}) copy-start(u32[256]{0:T(256)} %constant.61) | copy-start | bytes 3076
  185.9 14.4 %copy-start.1 = (s32[176]{0:T(256)S(1)}, s32[176]{0:T(256)}, u32[]{:S(2)}) copy-start(s32[176]{0:T(256)} %param.9) | copy-start | bytes 2116
  192.4 227.9 %all-gather.8.cloned.1.call-start = ((), (), s32[]{:S(2)}) async-start(), calls=%async_computation.3 | async-start | bytes 11894784 | tf_op jit(solution)/shard_map/all_gather | solution.py:91
Sparse Core Ops, SparseCore 0:
  17.3 161.1 all-gather.3
  192.6 115.8 all-gather.5
  311.3 109.0 all-gather.7
